TPU v7x, 32 devices: a whole 2x2x4 slice. The times are simulated.
32 devices in a mesh: groups: 2 (over y), dp: 4 (over z), section: 4 (over x, core).
Axes of the slice: x: 2, y: 2, z: 4, core: 2. Of those that a mesh axis runs over, the one named last changes fastest.
Arguments:
- activations: bfloat16 [4, 32, 16, 16, 512], P('section', ('groups', 'dp')), parts along dimension 1, may hold values from -6 to 6
- depth_small: float32 [4, 3, 3, 512], P('section'), may hold values from -2 to 2
- point_first: bfloat16 [4, 512, 512], P('section'), may hold values from -0.25 to 0.25
- depth_large: float32 [4, 5, 5, 512], P('section'), may hold values from -1.25 to 1.25
- point_second: bfloat16 [4, 512, 512], P('section'), may hold values from -0.25 to 0.25
- head_weight: bfloat16 [1000, 512], replicated, may hold values from -0.25 to 0.25
- offsets: int32 [32], P(('groups', 'dp')), parts along dimension 0, may hold values from 0 to 15
- labels: int32 [32], P(('groups', 'dp')), parts along dimension 0, may hold values from 0 to 999
Outputs:
- grad_first: float32 [4, 1024, 512], P('section', 'groups'), parts along dimension 1
- grad_second: float32 [4, 1024, 512], P('section', 'groups'), parts along dimension 1
- grad_small: float32 [4, 6, 3, 512], P('section', 'groups'), parts along dimension 1
- grad_large: float32 [4, 10, 5, 512], P('section', 'groups'), parts along dimension 1
There are 2 independent parts, one for each index of `groups`. A program takes and returns all parts, laid end to end along the dimension named above; an argument that names none is the same for every part. Nothing has to cross between parts.
All inputs are finite; a program needn't handle non-finite values.
Results may differ from a plain program's by a relative error of at most 0.0028.
Values may be sent and summed in bfloat16 or wider, within the bound.
A program may use at most 64 MiB of HBM per device.

v0:
```python
import jax
import jax.numpy as jnp
from jax import lax
from jax.sharding import PartitionSpec as P

BAND = 4
MICRO = 2


loss_scale = 64.0
contract_last = (((1,), (1,)), ((), ()))
contract_first = (((0,), (0,)), ((), ()))


def from_behind(block, axis, distance):
    devices = range(lax.axis_size(axis))
    route = [(i - distance, i) for i in devices if i - distance in devices]
    return lax.ppermute(block, axis, route)


def depth_conv(inputs, kernel):
    size = kernel.shape[0]
    radius = size // 2
    height, width = (inputs.shape[1], inputs.shape[2])
    padded = jnp.pad(inputs, ((0, 0), (radius, radius), (radius, radius), (0, 0)))
    result = jnp.zeros(inputs.shape, jnp.float32)
    for row_tap in range(size):
        for col_tap in range(size):
            result = (
                result
                + kernel[row_tap, col_tap]
                * padded[:, row_tap : row_tap + height, col_tap : col_tap + width, :]
            )
    return result


def depth_conv_t(grads, kernel):
    size = kernel.shape[0]
    radius = size // 2
    height, width = (grads.shape[1], grads.shape[2])
    padded = jnp.pad(grads, ((0, 0), (radius, radius), (radius, radius), (0, 0)))
    result = jnp.zeros(grads.shape, jnp.float32)
    for row_tap in range(size):
        for col_tap in range(size):
            row_start = 2 * radius - row_tap
            col_start = 2 * radius - col_tap
            result = (
                result
                + kernel[row_tap, col_tap]
                * padded[:, row_start : row_start + height, col_start : col_start + width, :]
            )
    return result


def depth_conv_k(inputs, grads, size):
    radius = size // 2
    height, width = (inputs.shape[1], inputs.shape[2])
    padded = jnp.pad(inputs, ((0, 0), (radius, radius), (radius, radius), (0, 0)))
    rows_out = []
    for row_tap in range(size):
        taps = []
        for col_tap in range(size):
            taps.append(
                jnp.sum(
                    padded[:, row_tap : row_tap + height, col_tap : col_tap + width, :] * grads,
                    axis=(0, 1, 2),
                )
            )
        rows_out.append(jnp.stack(taps))
    return jnp.stack(rows_out)


def per_device(
    activations, depth_small, point_first, depth_large, point_second, head_weight, offsets, labels
):
    section_index = lax.axis_index("section")
    section_count = lax.axis_size("section")
    stored = activations[0]
    images, height, width, chans = stored.shape
    kernel_small = depth_small[0]
    kernel_large = depth_large[0]
    weight_first = point_first[0]
    weight_second = point_second[0]
    columns = jnp.arange(width, dtype=jnp.int32)
    keep = (jnp.mod(columns[None, :] - offsets[:, None], width) < BAND).astype(jnp.float32)
    keep = jnp.where(section_index == 0, keep, 1.0)
    inputs = stored.astype(jnp.float32) * keep[:, None, :, None]
    first_act = jnp.maximum(inputs, 0.0)
    first_depth = depth_conv(first_act, kernel_small).astype(jnp.bfloat16)
    first_point = jnp.dot(
        first_depth.reshape(-1, chans), weight_first, preferred_element_type=jnp.float32
    )
    second_act = jnp.maximum(first_point, 0.0).astype(jnp.bfloat16).reshape(inputs.shape)
    second_depth = depth_conv(second_act.astype(jnp.float32), kernel_large).astype(jnp.bfloat16)
    second_point = jnp.dot(
        second_depth.reshape(-1, chans), weight_second, preferred_element_type=jnp.float32
    )
    pooled = jnp.mean(inputs + second_point.reshape(inputs.shape), axis=(1, 2))
    head_float = head_weight.astype(jnp.float32)
    logits = lax.dot_general(pooled, head_float, contract_last, precision=lax.Precision.HIGHEST)
    onehot = (labels[:, None] == jnp.arange(head_weight.shape[0], dtype=jnp.int32)[None, :]).astype(
        jnp.float32
    )
    grad_pool = jnp.dot(
        loss_scale * (logits - onehot), head_float, precision=lax.Precision.HIGHEST
    ) / (height * width)
    grad_last = jnp.broadcast_to(grad_pool[:, None, None, :], inputs.shape).astype(jnp.bfloat16)
    pieces = MICRO
    piece_len = images // pieces
    steps_total = section_count + pieces - 1

    def take(array, piece_num):
        return lax.dynamic_slice_in_dim(array, piece_num * piece_len, piece_len, 0)

    def one_step(step_num, carry):
        received, stores = carry
        piece_num = step_num - (section_count - 1 - section_index)
        valid = jnp.logical_and(piece_num >= 0, piece_num < pieces)
        piece_num = jnp.clip(piece_num, 0, pieces - 1)
        grad_out = jnp.where(
            section_index == section_count - 1, take(grad_last, piece_num), received
        )
        part_inputs = take(inputs, piece_num)
        part_act2 = take(second_act, piece_num)
        grad_rows = grad_out.reshape(-1, chans)
        grad_depth2 = lax.dot_general(
            grad_rows, weight_second, contract_last, preferred_element_type=jnp.float32
        ).reshape(part_inputs.shape)
        back_act2 = depth_conv_t(grad_depth2, kernel_large)
        grad_point1 = jnp.where(part_act2 > 0, back_act2, 0.0).astype(jnp.bfloat16)
        point_rows = grad_point1.reshape(-1, chans)
        grad_depth1 = lax.dot_general(
            point_rows, weight_first, contract_last, preferred_element_type=jnp.float32
        ).reshape(part_inputs.shape)
        back_act1 = depth_conv_t(grad_depth1, kernel_small)
        grad_in = (
            grad_out.astype(jnp.float32) + jnp.where(part_inputs > 0, back_act1, 0.0)
        ).astype(jnp.bfloat16)
        sent = from_behind(grad_in, "section", -1)
        acc_first, acc_second, acc_small, acc_large = stores
        part_depth1 = take(first_depth, piece_num).reshape(-1, chans)
        part_depth2 = take(second_depth, piece_num).reshape(-1, chans)
        scale_live = jnp.where(valid, 1.0, 0.0)
        acc_second = acc_second + scale_live * lax.dot_general(
            part_depth2, grad_rows, contract_first, preferred_element_type=jnp.float32
        )
        acc_first = acc_first + scale_live * lax.dot_general(
            part_depth1, point_rows, contract_first, preferred_element_type=jnp.float32
        )
        acc_large = acc_large + scale_live * depth_conv_k(
            part_act2.astype(jnp.float32), grad_depth2, 5
        )
        acc_small = acc_small + scale_live * depth_conv_k(
            jnp.maximum(part_inputs, 0.0), grad_depth1, 3
        )
        stores = (acc_first, acc_second, acc_small, acc_large)
        return (sent, stores)

    start_recv = jnp.zeros((piece_len, height, width, chans), jnp.bfloat16)
    start_stores = (
        jnp.zeros((chans, chans), jnp.float32),
        jnp.zeros((chans, chans), jnp.float32),
        jnp.zeros((3, 3, chans), jnp.float32),
        jnp.zeros((5, 5, chans), jnp.float32),
    )
    final_recv, totals = lax.fori_loop(0, steps_total, one_step, (start_recv, start_stores))
    sum_first, sum_second, sum_small, sum_large = totals
    sum_first, sum_second, sum_small, sum_large = lax.psum(
        (sum_first, sum_second, sum_small, sum_large), "dp"
    )
    return (sum_first[None], sum_second[None], sum_small[None], sum_large[None])


def solution(mesh):
    placed = (
        P("section", ("groups", "dp"), None, None, None),
        P("section", None, None, None),
        P("section", None, None),
        P("section", None, None, None),
        P("section", None, None),
        P(),
        P(("groups", "dp")),
        P(("groups", "dp")),
    )
    return jax.shard_map(
        per_device,
        mesh=mesh,
        in_specs=placed,
        out_specs=(
            P("section", "groups", None),
            P("section", "groups", None),
            P("section", "groups", None, None),
            P("section", "groups", None, None),
        ),
        check_vma=False,
    )
```

profile of v0, /device:TPU:0, one launch (start us, length us, event | category | flops | bytes accessed | tf_op | source)
XLA Modules:
  0.0 297.4 jit_solution(16423216276230622938)
XLA Ops:
  7.2 0.9 copy.21
  8.2 0.7 copy.22
  9.0 0.7 convert_select_fusion
  9.7 3.2 %convert_multiply_fusion = (f32[4,16,16,512]{3,2,1,0:T(8,128)}, f32[4,16,16,512]{3,2,1,0:T(8,128)S(1)}) fusion(bf16[1,4,16,16,512]{4,3,2,1,0:T(8,128)(2,1)} %param.10, f32[4,16]{1,0:T(4,128)S(1)} %convert_select_fusion), kind=kLoop, calls=%fused_computation.325 | loop fusion | flops 1572864 | bytes 5243136 | tf_op jit(solution)/shard_map/mul | solution.py:87
  12.9 2.9 fusion.155
  15.8 0.7 maximum_convert_fusion
  16.9 6.3 %fusion.210 = bf16[4,16,16,512]{3,2,1,0:T(8,128)(2,1)S(1)} fusion(f32[4,16,16,512]{3,2,1,0:T(8,128)S(1)} %convert_element_type.94, f32[512]{0:T(512)S(1)} %bitcast.436, f32[512]{0:T(512)S(1)} %bitcast.437, f32[512]{0:T(512)S(1)} %bitcast.438, f32[512]{0:T(512)S(1)} %bitcast.439, f32[512]{0:T(512)S(1)} %bitcast.440, f32[512]{0:T(512)S(1)} %bitcast.441, ...), kind=kLoop, calls=%fused_computation.323 | loop fusion | flops 26214400 | bytes 3196928 | tf_op jit(solution)/shard_map/convert_element_type | solution.py:94
  23.2 0.7 add_reduce_fusion
  24.2 0.9 fusion.212
  25.6 1.1 broadcast_in_dim.39
  26.7 0.9 broadcast.95
  27.6 125.3 %while.24 = (s32[]{:T(128)}, bf16[2,16,16,512]{3,2,1,0:T(8,128)(2,1)}, f32[512,512]{1,0:T(8,128)}, f32[512,512]{1,0:T(8,128)}, f32[3,3,512]{2,1,0:T(4,128)S(1)},...) while((s32[]{:T(128)}, ...), condition=%wide.region_36.37_spmd.clone, body=%wide.region_1.36_spmd.clone.sunk | while | flops 1113640960 | bytes 74709792 | solution.py:166
  27.7 1.7 dynamic-slice_select_fusion.2
  29.4 2.4 fusion.261
  31.8 3.4 %fusion.263 = bf16[2,16,16,512]{3,2,1,0:T(8,128)(2,1)S(1)} fusion(f32[2,16,16,512]{3,2,1,0:T(8,128)S(1)} %get-tuple-element.784, f32[512]{0:T(512)S(1)} %bitcast.380, f32[512]{0:T(512)S(1)} %bitcast.381, f32[512]{0:T(512)S(1)} %bitcast.382, f32[512]{0:T(512)S(1)} %bitcast.383, f32[512]{0:T(512)S(1)} %bitcast.384, f32[512]{0:T(512)S(1)} %bitcast.385, ...), kind=kLoop, calls=%fused_computation.152.clone.1 | loop fusion | flops 13631488 | bytes 2148356 | tf_op jit(solution)/shard_map/while/body/eval_jaxpr/convert_element_type | solution.py:130
  35.7 2.0 dynamic-slice_maximum_fusion.2
  37.8 1.3 collective-permute-start
  39.1 3.3 %fusion.269 = (f32[512]{0:T(512)S(1)}, f32[512]{0:T(512)S(1)}, f32[512]{0:T(512)S(1)}, f32[512]{0:T(512)S(1)}, f32[512]{0:T(512)S(1)}, /*index=5*/f32[512]{0:T(5...) fusion(f32[2,16,16,512]{3,2,1,0:T(8,128)} %copy-done.1, ...), kind=kLoop, calls=%fused_computation.201.clone.1 | loop fusion | flops 9427968 | bytes 2134016 | tf_op jit(solution)/shard_map/while/body/eval_jaxpr/reduce_sum | solution.py:64
  42.4 5.4 %fusion.267 = (f32[512]{0:T(512)S(1)}, f32[512]{0:T(512)S(1)}, f32[512]{0:T(512)S(1)}, f32[512]{0:T(512)S(1)}, f32[512]{0:T(512)S(1)}, /*index=5*/f32[512]{0:T(5...) fusion(f32[2,16,16,512]{3,2,1,0:T(8,128)S(1)} %fusion.264, f32[2,16,16,512]{3,2,1,0:T(8,128)} %get-tuple-element.816), kind=kLoop, calls=%fused_computation.89.clone.1 | loop fusion | flops 4713984 | bytes 2115584 | tf_op jit(solution)/shard_map/while/body/eval_jaxpr/reduce_sum | solution.py:64
  48.0 2.6 fusion.266
  51.4 0.9 copy-done.13
  52.5 1.7 dynamic-slice_select_fusion.2
  54.2 2.4 fusion.261
  56.6 3.4 %fusion.263 = bf16[2,16,16,512]{3,2,1,0:T(8,128)(2,1)S(1)} fusion(f32[2,16,16,512]{3,2,1,0:T(8,128)S(1)} %get-tuple-element.784, f32[512]{0:T(512)S(1)} %bitcast.380, f32[512]{0:T(512)S(1)} %bitcast.381, f32[512]{0:T(512)S(1)} %bitcast.382, f32[512]{0:T(512)S(1)} %bitcast.383, f32[512]{0:T(512)S(1)} %bitcast.384, f32[512]{0:T(512)S(1)} %bitcast.385, ...), kind=kLoop, calls=%fused_computation.152.clone.1 | loop fusion | flops 13631488 | bytes 2148356 | tf_op jit(solution)/shard_map/while/body/eval_jaxpr/convert_element_type | solution.py:130
  60.5 2.0 dynamic-slice_maximum_fusion.2
  62.6 1.3 collective-permute-start
  63.9 3.3 %fusion.269 = (f32[512]{0:T(512)S(1)}, f32[512]{0:T(512)S(1)}, f32[512]{0:T(512)S(1)}, f32[512]{0:T(512)S(1)}, f32[512]{0:T(512)S(1)}, /*index=5*/f32[512]{0:T(5...) fusion(f32[2,16,16,512]{3,2,1,0:T(8,128)} %copy-done.1, ...), kind=kLoop, calls=%fused_computation.201.clone.1 | loop fusion | flops 9427968 | bytes 2134016 | tf_op jit(solution)/shard_map/while/body/eval_jaxpr/reduce_sum | solution.py:64
  67.2 5.4 %fusion.267 = (f32[512]{0:T(512)S(1)}, f32[512]{0:T(512)S(1)}, f32[512]{0:T(512)S(1)}, f32[512]{0:T(512)S(1)}, f32[512]{0:T(512)S(1)}, /*index=5*/f32[512]{0:T(5...) fusion(f32[2,16,16,512]{3,2,1,0:T(8,128)S(1)} %fusion.264, f32[2,16,16,512]{3,2,1,0:T(8,128)} %get-tuple-element.816), kind=kLoop, calls=%fused_computation.89.clone.1 | loop fusion | flops 4713984 | bytes 2115584 | tf_op jit(solution)/shard_map/while/body/eval_jaxpr/reduce_sum | solution.py:64
  72.8 3.0 %fusion.266 = f32[512,512]{1,0:T(8,128)} fusion(bf16[2,16,16,512]{3,2,1,0:T(8,128)(2,1)S(1)} %copy-done.5, f32[512,512]{1,0:T(8,128)} %get-tuple-element.877, bf16[4,16,16,512]{3,2,1,0:T(8,128)(2,1)} %get-tuple-element.913, s32[]{:T(128)S(6)} %select_n.125, f32[]{:T(128)S(6)} %select_n.126, pred[]{:T(512)S(6)} %compare.13), kind=kOutput, calls=%fused_computation.68.clone.1 | convolution fusion | flops 269221888 | bytes 3145737 | tf_op jit(solution)/shard_map/while/body/eval_jaxpr/dot_general | solution.py:144
  76.6 0.9 copy-done.13
  77.6 1.7 dynamic-slice_select_fusion.2
  79.3 2.4 fusion.261
  81.7 3.4 %fusion.263 = bf16[2,16,16,512]{3,2,1,0:T(8,128)(2,1)S(1)} fusion(f32[2,16,16,512]{3,2,1,0:T(8,128)S(1)} %get-tuple-element.784, f32[512]{0:T(512)S(1)} %bitcast.380, f32[512]{0:T(512)S(1)} %bitcast.381, f32[512]{0:T(512)S(1)} %bitcast.382, f32[512]{0:T(512)S(1)} %bitcast.383, f32[512]{0:T(512)S(1)} %bitcast.384, f32[512]{0:T(512)S(1)} %bitcast.385, ...), kind=kLoop, calls=%fused_computation.152.clone.1 | loop fusion | flops 13631488 | bytes 2148356 | tf_op jit(solution)/shard_map/while/body/eval_jaxpr/convert_element_type | solution.py:130
  85.6 2.0 dynamic-slice_maximum_fusion.2
  87.7 1.3 collective-permute-start
  89.0 3.3 %fusion.269 = (f32[512]{0:T(512)S(1)}, f32[512]{0:T(512)S(1)}, f32[512]{0:T(512)S(1)}, f32[512]{0:T(512)S(1)}, f32[512]{0:T(512)S(1)}, /*index=5*/f32[512]{0:T(5...) fusion(f32[2,16,16,512]{3,2,1,0:T(8,128)} %copy-done.1, ...), kind=kLoop, calls=%fused_computation.201.clone.1 | loop fusion | flops 9427968 | bytes 2134016 | tf_op jit(solution)/shard_map/while/body/eval_jaxpr/reduce_sum | solution.py:64
  92.4 5.4 %fusion.267 = (f32[512]{0:T(512)S(1)}, f32[512]{0:T(512)S(1)}, f32[512]{0:T(512)S(1)}, f32[512]{0:T(512)S(1)}, f32[512]{0:T(512)S(1)}, /*index=5*/f32[512]{0:T(5...) fusion(f32[2,16,16,512]{3,2,1,0:T(8,128)S(1)} %fusion.264, f32[2,16,16,512]{3,2,1,0:T(8,128)} %get-tuple-element.816), kind=kLoop, calls=%fused_computation.89.clone.1 | loop fusion | flops 4713984 | bytes 2115584 | tf_op jit(solution)/shard_map/while/body/eval_jaxpr/reduce_sum | solution.py:64
  97.9 3.0 %fusion.266 = f32[512,512]{1,0:T(8,128)} fusion(bf16[2,16,16,512]{3,2,1,0:T(8,128)(2,1)S(1)} %copy-done.5, f32[512,512]{1,0:T(8,128)} %get-tuple-element.877, bf16[4,16,16,512]{3,2,1,0:T(8,128)(2,1)} %get-tuple-element.913, s32[]{:T(128)S(6)} %select_n.125, f32[]{:T(128)S(6)} %select_n.126, pred[]{:T(512)S(6)} %compare.13), kind=kOutput, calls=%fused_computation.68.clone.1 | convolution fusion | flops 269221888 | bytes 3145737 | tf_op jit(solution)/shard_map/while/body/eval_jaxpr/dot_general | solution.py:144
  101.7 0.9 copy-done.13
  102.7 1.7 dynamic-slice_select_fusion.2
  104.4 2.4 fusion.261
  106.8 3.4 %fusion.263 = bf16[2,16,16,512]{3,2,1,0:T(8,128)(2,1)S(1)} fusion(f32[2,16,16,512]{3,2,1,0:T(8,128)S(1)} %get-tuple-element.784, f32[512]{0:T(512)S(1)} %bitcast.380, f32[512]{0:T(512)S(1)} %bitcast.381, f32[512]{0:T(512)S(1)} %bitcast.382, f32[512]{0:T(512)S(1)} %bitcast.383, f32[512]{0:T(512)S(1)} %bitcast.384, f32[512]{0:T(512)S(1)} %bitcast.385, ...), kind=kLoop, calls=%fused_computation.152.clone.1 | loop fusion | flops 13631488 | bytes 2148356 | tf_op jit(solution)/shard_map/while/body/eval_jaxpr/convert_element_type | solution.py:130
  110.8 2.0 dynamic-slice_maximum_fusion.2
  112.8 1.3 collective-permute-start
  114.1 3.3 %fusion.269 = (f32[512]{0:T(512)S(1)}, f32[512]{0:T(512)S(1)}, f32[512]{0:T(512)S(1)}, f32[512]{0:T(512)S(1)}, f32[512]{0:T(512)S(1)}, /*index=5*/f32[512]{0:T(5...) fusion(f32[2,16,16,512]{3,2,1,0:T(8,128)} %copy-done.1, ...), kind=kLoop, calls=%fused_computation.201.clone.1 | loop fusion | flops 9427968 | bytes 2134016 | tf_op jit(solution)/shard_map/while/body/eval_jaxpr/reduce_sum | solution.py:64
  117.5 5.4 %fusion.267 = (f32[512]{0:T(512)S(1)}, f32[512]{0:T(512)S(1)}, f32[512]{0:T(512)S(1)}, f32[512]{0:T(512)S(1)}, f32[512]{0:T(512)S(1)}, /*index=5*/f32[512]{0:T(5...) fusion(f32[2,16,16,512]{3,2,1,0:T(8,128)S(1)} %fusion.264, f32[2,16,16,512]{3,2,1,0:T(8,128)} %get-tuple-element.816), kind=kLoop, calls=%fused_computation.89.clone.1 | loop fusion | flops 4713984 | bytes 2115584 | tf_op jit(solution)/shard_map/while/body/eval_jaxpr/reduce_sum | solution.py:64
  123.1 3.0 %fusion.266 = f32[512,512]{1,0:T(8,128)} fusion(bf16[2,16,16,512]{3,2,1,0:T(8,128)(2,1)S(1)} %copy-done.5, f32[512,512]{1,0:T(8,128)} %get-tuple-element.877, bf16[4,16,16,512]{3,2,1,0:T(8,128)(2,1)} %get-tuple-element.913, s32[]{:T(128)S(6)} %select_n.125, f32[]{:T(128)S(6)} %select_n.126, pred[]{:T(512)S(6)} %compare.13), kind=kOutput, calls=%fused_computation.68.clone.1 | convolution fusion | flops 269221888 | bytes 3145737 | tf_op jit(solution)/shard_map/while/body/eval_jaxpr/dot_general | solution.py:144
  126.8 0.9 copy-done.13
  127.9 1.7 dynamic-slice_select_fusion.2
  129.6 2.4 fusion.261
  132.0 3.4 %fusion.263 = bf16[2,16,16,512]{3,2,1,0:T(8,128)(2,1)S(1)} fusion(f32[2,16,16,512]{3,2,1,0:T(8,128)S(1)} %get-tuple-element.784, f32[512]{0:T(512)S(1)} %bitcast.380, f32[512]{0:T(512)S(1)} %bitcast.381, f32[512]{0:T(512)S(1)} %bitcast.382, f32[512]{0:T(512)S(1)} %bitcast.383, f32[512]{0:T(512)S(1)} %bitcast.384, f32[512]{0:T(512)S(1)} %bitcast.385, ...), kind=kLoop, calls=%fused_computation.152.clone.1 | loop fusion | flops 13631488 | bytes 2148356 | tf_op jit(solution)/shard_map/while/body/eval_jaxpr/convert_element_type | solution.py:130
  135.9 2.0 dynamic-slice_maximum_fusion.2
  138.0 1.3 collective-permute-start
  139.3 3.3 %fusion.269 = (f32[512]{0:T(512)S(1)}, f32[512]{0:T(512)S(1)}, f32[512]{0:T(512)S(1)}, f32[512]{0:T(512)S(1)}, f32[512]{0:T(512)S(1)}, /*index=5*/f32[512]{0:T(5...) fusion(f32[2,16,16,512]{3,2,1,0:T(8,128)} %copy-done.1, ...), kind=kLoop, calls=%fused_computation.201.clone.1 | loop fusion | flops 9427968 | bytes 2134016 | tf_op jit(solution)/shard_map/while/body/eval_jaxpr/reduce_sum | solution.py:64
  142.6 5.4 %fusion.267 = (f32[512]{0:T(512)S(1)}, f32[512]{0:T(512)S(1)}, f32[512]{0:T(512)S(1)}, f32[512]{0:T(512)S(1)}, f32[512]{0:T(512)S(1)}, /*index=5*/f32[512]{0:T(5...) fusion(f32[2,16,16,512]{3,2,1,0:T(8,128)S(1)} %fusion.264, f32[2,16,16,512]{3,2,1,0:T(8,128)} %get-tuple-element.816), kind=kLoop, calls=%fused_computation.89.clone.1 | loop fusion | flops 4713984 | bytes 2115584 | tf_op jit(solution)/shard_map/while/body/eval_jaxpr/reduce_sum | solution.py:64
  148.2 3.0 %fusion.266 = f32[512,512]{1,0:T(8,128)} fusion(bf16[2,16,16,512]{3,2,1,0:T(8,128)(2,1)S(1)} %copy-done.5, f32[512,512]{1,0:T(8,128)} %get-tuple-element.877, bf16[4,16,16,512]{3,2,1,0:T(8,128)(2,1)} %get-tuple-element.913, s32[]{:T(128)S(6)} %select_n.125, f32[]{:T(128)S(6)} %select_n.126, pred[]{:T(512)S(6)} %compare.13), kind=kOutput, calls=%fused_computation.68.clone.1 | convolution fusion | flops 269221888 | bytes 3145737 | tf_op jit(solution)/shard_map/while/body/eval_jaxpr/dot_general | solution.py:144
  152.0 0.9 copy-done.13
  153.6 0.7 broadcast_in_dim.43
  154.3 0.7 all-reduce.13.cloned.1.call-update
  155.0 40.8 %all-reduce.11.cloned.1.call-done = (f32[1,3,3,512]{3,0,2,1:T(1,128)}, f32[1,5,5,512]{3,0,2,1:T(1,128)}) async-done(((f32[1,3,3,512]{3,0,2,1:T(1,128)}, f32[1,5,5,512]{3,0,2,1:T(1,128)}), (f32[1,3,3,512]{3,0,2,1:T(1,128)}, f32[1,5,5,512]{3,0,2,1:T(1,128)})) %all-reduce.11.cloned.1.call-update) | async-done | bytes 69648 | tf_op jit(solution)/shard_map/psum | solution.py:168
  195.8 90.2 %all-reduce.13.cloned.1.call-done = (f32[1,512,512]{2,1,0:T(8,128)}, f32[1,512,512]{2,1,0:T(8,128)}) async-done(((f32[1,512,512]{2,1,0:T(8,128)}, f32[1,512,512]{2,1,0:T(8,128)}), (f32[1,512,512]{2,1,0:T(8,128)}, f32[1,512,512]{2,1,0:T(8,128)})) %all-reduce.13.cloned.1.call-update) | async-done | bytes 2097168 | tf_op jit(solution)/shard_map/psum | solution.py:168
  286.0 2.3 copy.49
  288.4 1.0 copy.50
  290.0 0.6 copy.52
  (259 shorter events, 9.6 us)
Async XLA Ops:
  7.2 17.0 %copy-start = (bf16[1000,512]{1,0:T(8,128)(2,1)S(1)}, bf16[1000,512]{1,0:T(8,128)(2,1)}, u32[]{:S(2)}) copy-start(bf16[1000,512]{1,0:T(8,128)(2,1)} %param.15) | copy-start | bytes 3072004
  7.2 188.7 %all-reduce.11.cloned.1.call-start = ((), (), s32[]{:S(2)}) async-start(), calls=%async_computation | async-start | bytes 139264 | tf_op jit(solution)/shard_map/psum | solution.py:168
  12.9 2.9 copy-start.9
  16.9 6.3 %copy-start.11 = (bf16[1,4,16,16,512]{4,3,2,1,0:T(8,128)(2,1)S(1)}, bf16[1,4,16,16,512]{4,3,2,1,0:T(8,128)(2,1)}, u32[]{:S(2)}) copy-start(bf16[1,4,16,16,512]{4,3,2,1,0:T(8,128)(2,1)} %param.10) | copy-start | bytes 3145732
  16.9 6.3 %copy-start.21 = (bf16[1,512,512]{2,1,0:T(8,128)(2,1)S(1)}, bf16[1,512,512]{2,1,0:T(8,128)(2,1)}, u32[]{:S(2)}) copy-start(bf16[1,512,512]{2,1,0:T(8,128)(2,1)} %param.14) | copy-start | bytes 1572868
  27.6 4.2 %copy-start.6 = (bf16[4,16,16,512]{3,2,1,0:T(8,128)(2,1)}, bf16[4,16,16,512]{3,2,1,0:T(8,128)(2,1)S(1)}, u32[]{:S(2)}) copy-start(bf16[4,16,16,512]{3,2,1,0:T(8,128)(2,1)S(1)} %get-tuple-element.908) | copy-start | bytes 3145732 | tf_op jit(solution)/shard_map/while
  29.4 6.3 %copy-start.4 = (bf16[2,16,16,512]{3,2,1,0:T(8,128)(2,1)}, bf16[2,16,16,512]{3,2,1,0:T(8,128)(2,1)S(1)}, u32[]{:S(2)}) copy-start(bf16[2,16,16,512]{3,2,1,0:T(8,128)(2,1)S(1)} %get-tuple-element.783) | copy-start | bytes 1572868 | tf_op jit(solution)/shard_map/while
  31.7 4.0 %copy-start.1 = (f32[2,16,16,512]{3,2,1,0:T(8,128)}, f32[2,16,16,512]{3,2,1,0:T(8,128)S(1)}, u32[]{:S(2)}) copy-start(f32[2,16,16,512]{3,2,1,0:T(8,128)S(1)} %get-tuple-element.784) | copy-start | bytes 3145732 | tf_op jit(solution)/shard_map/while
  31.7 3.5 %copy-start.10 = (bf16[512,512]{1,0:T(8,128)(2,1)S(1)}, bf16[512,512]{1,0:T(8,128)(2,1)}, u32[]{:S(2)}) copy-start(bf16[512,512]{1,0:T(8,128)(2,1)} %get-tuple-element.911) | copy-start | bytes 1572868 | tf_op jit(solution)/shard_map/while
  31.8 3.9 %copy-start.8 = (f32[4,16,16,512]{3,2,1,0:T(8,128)S(1)}, f32[4,16,16,512]{3,2,1,0:T(8,128)}, u32[]{:S(2)}) copy-start(f32[4,16,16,512]{3,2,1,0:T(8,128)} %get-tuple-element.906) | copy-start | bytes 6291460 | tf_op jit(solution)/shard_map/while
  35.2 2.6 copy-start.2
  37.8 13.7 %collective-permute-start = (bf16[2,16,16,512]{3,2,1,0:T(8,128)(2,1)}, bf16[2,16,16,512]{3,2,1,0:T(8,128)(2,1)}, u32[]{:S(2)}, u32[]{:S(2)}) collective-permute-start(bf16[2,16,16,512]{3,2,1,0:T(8,128)(2,1)} %get-tuple-element.815), channel_id=1, source_target_pairs={{1,0},{2,1},{3,2},{5,4},{6,5},{7,6},{9,8},{10,9},{11,10},{13,12},{... | collective-permute-start | bytes 1572872 | tf_op jit(solution)/shard_map/while/body/eval_jaxpr/ppermute | solution.py:18
  42.4 5.6 %copy-start.5 = (bf16[2,16,16,512]{3,2,1,0:T(8,128)(2,1)S(1)}, bf16[2,16,16,512]{3,2,1,0:T(8,128)(2,1)}, u32[]{:S(2)}) copy-start(bf16[2,16,16,512]{3,2,1,0:T(8,128)(2,1)} %copy-done.4) | copy-start | bytes 1572868 | tf_op jit(solution)/shard_map/while
  48.0 2.8 copy-start.3
  48.0 2.8 copy-start.12
  48.0 2.8 copy-start.16
  52.4 4.2 %copy-start.6 = (bf16[4,16,16,512]{3,2,1,0:T(8,128)(2,1)}, bf16[4,16,16,512]{3,2,1,0:T(8,128)(2,1)S(1)}, u32[]{:S(2)}) copy-start(bf16[4,16,16,512]{3,2,1,0:T(8,128)(2,1)S(1)} %get-tuple-element.908) | copy-start | bytes 3145732 | tf_op jit(solution)/shard_map/while
  54.1 6.3 %copy-start.4 = (bf16[2,16,16,512]{3,2,1,0:T(8,128)(2,1)}, bf16[2,16,16,512]{3,2,1,0:T(8,128)(2,1)S(1)}, u32[]{:S(2)}) copy-start(bf16[2,16,16,512]{3,2,1,0:T(8,128)(2,1)S(1)} %get-tuple-element.783) | copy-start | bytes 1572868 | tf_op jit(solution)/shard_map/while
  56.5 4.0 %copy-start.1 = (f32[2,16,16,512]{3,2,1,0:T(8,128)}, f32[2,16,16,512]{3,2,1,0:T(8,128)S(1)}, u32[]{:S(2)}) copy-start(f32[2,16,16,512]{3,2,1,0:T(8,128)S(1)} %get-tuple-element.784) | copy-start | bytes 3145732 | tf_op jit(solution)/shard_map/while
  56.5 3.5 %copy-start.10 = (bf16[512,512]{1,0:T(8,128)(2,1)S(1)}, bf16[512,512]{1,0:T(8,128)(2,1)}, u32[]{:S(2)}) copy-start(bf16[512,512]{1,0:T(8,128)(2,1)} %get-tuple-element.911) | copy-start | bytes 1572868 | tf_op jit(solution)/shard_map/while
  56.6 3.9 %copy-start.8 = (f32[4,16,16,512]{3,2,1,0:T(8,128)S(1)}, f32[4,16,16,512]{3,2,1,0:T(8,128)}, u32[]{:S(2)}) copy-start(f32[4,16,16,512]{3,2,1,0:T(8,128)} %get-tuple-element.906) | copy-start | bytes 6291460 | tf_op jit(solution)/shard_map/while
  60.0 2.6 copy-start.2
  62.6 14.0 %collective-permute-start = (bf16[2,16,16,512]{3,2,1,0:T(8,128)(2,1)}, bf16[2,16,16,512]{3,2,1,0:T(8,128)(2,1)}, u32[]{:S(2)}, u32[]{:S(2)}) collective-permute-start(bf16[2,16,16,512]{3,2,1,0:T(8,128)(2,1)} %get-tuple-element.815), channel_id=1, source_target_pairs={{1,0},{2,1},{3,2},{5,4},{6,5},{7,6},{9,8},{10,9},{11,10},{13,12},{... | collective-permute-start | bytes 1572872 | tf_op jit(solution)/shard_map/while/body/eval_jaxpr/ppermute | solution.py:18
  67.2 5.6 %copy-start.5 = (bf16[2,16,16,512]{3,2,1,0:T(8,128)(2,1)S(1)}, bf16[2,16,16,512]{3,2,1,0:T(8,128)(2,1)}, u32[]{:S(2)}) copy-start(bf16[2,16,16,512]{3,2,1,0:T(8,128)(2,1)} %copy-done.4) | copy-start | bytes 1572868 | tf_op jit(solution)/shard_map/while
  72.8 3.1 %copy-start.3 = (bf16[2,16,16,512]{3,2,1,0:T(8,128)(2,1)S(1)}, bf16[2,16,16,512]{3,2,1,0:T(8,128)(2,1)}, u32[]{:S(2)}) copy-start(bf16[2,16,16,512]{3,2,1,0:T(8,128)(2,1)} %copy-done.2) | copy-start | bytes 1572868 | tf_op jit(solution)/shard_map/while
  72.8 3.1 %copy-start.12 = (f32[512,512]{1,0:T(8,128)S(1)}, f32[512,512]{1,0:T(8,128)}, u32[]{:S(2)}) copy-start(f32[512,512]{1,0:T(8,128)} %get-tuple-element.876) | copy-start | bytes 3145732 | tf_op jit(solution)/shard_map/while
  72.8 3.1 %copy-start.16 = (bf16[4,16,16,512]{3,2,1,0:T(8,128)(2,1)S(1)}, bf16[4,16,16,512]{3,2,1,0:T(8,128)(2,1)}, u32[]{:S(2)}) copy-start(bf16[4,16,16,512]{3,2,1,0:T(8,128)(2,1)} %get-tuple-element.912) | copy-start | bytes 3145732 | tf_op jit(solution)/shard_map/while
  77.5 4.2 %copy-start.6 = (bf16[4,16,16,512]{3,2,1,0:T(8,128)(2,1)}, bf16[4,16,16,512]{3,2,1,0:T(8,128)(2,1)S(1)}, u32[]{:S(2)}) copy-start(bf16[4,16,16,512]{3,2,1,0:T(8,128)(2,1)S(1)} %get-tuple-element.908) | copy-start | bytes 3145732 | tf_op jit(solution)/shard_map/while
  79.3 6.3 %copy-start.4 = (bf16[2,16,16,512]{3,2,1,0:T(8,128)(2,1)}, bf16[2,16,16,512]{3,2,1,0:T(8,128)(2,1)S(1)}, u32[]{:S(2)}) copy-start(bf16[2,16,16,512]{3,2,1,0:T(8,128)(2,1)S(1)} %get-tuple-element.783) | copy-start | bytes 1572868 | tf_op jit(solution)/shard_map/while
  81.7 4.0 %copy-start.1 = (f32[2,16,16,512]{3,2,1,0:T(8,128)}, f32[2,16,16,512]{3,2,1,0:T(8,128)S(1)}, u32[]{:S(2)}) copy-start(f32[2,16,16,512]{3,2,1,0:T(8,128)S(1)} %get-tuple-element.784) | copy-start | bytes 3145732 | tf_op jit(solution)/shard_map/while
  81.7 3.5 %copy-start.10 = (bf16[512,512]{1,0:T(8,128)(2,1)S(1)}, bf16[512,512]{1,0:T(8,128)(2,1)}, u32[]{:S(2)}) copy-start(bf16[512,512]{1,0:T(8,128)(2,1)} %get-tuple-element.911) | copy-start | bytes 1572868 | tf_op jit(solution)/shard_map/while
  81.7 3.9 %copy-start.8 = (f32[4,16,16,512]{3,2,1,0:T(8,128)S(1)}, f32[4,16,16,512]{3,2,1,0:T(8,128)}, u32[]{:S(2)}) copy-start(f32[4,16,16,512]{3,2,1,0:T(8,128)} %get-tuple-element.906) | copy-start | bytes 6291460 | tf_op jit(solution)/shard_map/while
  85.1 2.6 copy-start.2
  87.7 14.0 %collective-permute-start = (bf16[2,16,16,512]{3,2,1,0:T(8,128)(2,1)}, bf16[2,16,16,512]{3,2,1,0:T(8,128)(2,1)}, u32[]{:S(2)}, u32[]{:S(2)}) collective-permute-start(bf16[2,16,16,512]{3,2,1,0:T(8,128)(2,1)} %get-tuple-element.815), channel_id=1, source_target_pairs={{1,0},{2,1},{3,2},{5,4},{6,5},{7,6},{9,8},{10,9},{11,10},{13,12},{... | collective-permute-start | bytes 1572872 | tf_op jit(solution)/shard_map/while/body/eval_jaxpr/ppermute | solution.py:18
  92.3 5.6 %copy-start.5 = (bf16[2,16,16,512]{3,2,1,0:T(8,128)(2,1)S(1)}, bf16[2,16,16,512]{3,2,1,0:T(8,128)(2,1)}, u32[]{:S(2)}) copy-start(bf16[2,16,16,512]{3,2,1,0:T(8,128)(2,1)} %copy-done.4) | copy-start | bytes 1572868 | tf_op jit(solution)/shard_map/while
  97.9 3.1 %copy-start.3 = (bf16[2,16,16,512]{3,2,1,0:T(8,128)(2,1)S(1)}, bf16[2,16,16,512]{3,2,1,0:T(8,128)(2,1)}, u32[]{:S(2)}) copy-start(bf16[2,16,16,512]{3,2,1,0:T(8,128)(2,1)} %copy-done.2) | copy-start | bytes 1572868 | tf_op jit(solution)/shard_map/while
  97.9 3.1 %copy-start.12 = (f32[512,512]{1,0:T(8,128)S(1)}, f32[512,512]{1,0:T(8,128)}, u32[]{:S(2)}) copy-start(f32[512,512]{1,0:T(8,128)} %get-tuple-element.876) | copy-start | bytes 3145732 | tf_op jit(solution)/shard_map/while
  97.9 3.1 %copy-start.16 = (bf16[4,16,16,512]{3,2,1,0:T(8,128)(2,1)S(1)}, bf16[4,16,16,512]{3,2,1,0:T(8,128)(2,1)}, u32[]{:S(2)}) copy-start(bf16[4,16,16,512]{3,2,1,0:T(8,128)(2,1)} %get-tuple-element.912) | copy-start | bytes 3145732 | tf_op jit(solution)/shard_map/while
  102.7 4.2 %copy-start.6 = (bf16[4,16,16,512]{3,2,1,0:T(8,128)(2,1)}, bf16[4,16,16,512]{3,2,1,0:T(8,128)(2,1)S(1)}, u32[]{:S(2)}) copy-start(bf16[4,16,16,512]{3,2,1,0:T(8,128)(2,1)S(1)} %get-tuple-element.908) | copy-start | bytes 3145732 | tf_op jit(solution)/shard_map/while
  104.4 6.3 %copy-start.4 = (bf16[2,16,16,512]{3,2,1,0:T(8,128)(2,1)}, bf16[2,16,16,512]{3,2,1,0:T(8,128)(2,1)S(1)}, u32[]{:S(2)}) copy-start(bf16[2,16,16,512]{3,2,1,0:T(8,128)(2,1)S(1)} %get-tuple-element.783) | copy-start | bytes 1572868 | tf_op jit(solution)/shard_map/while
  106.8 4.0 %copy-start.1 = (f32[2,16,16,512]{3,2,1,0:T(8,128)}, f32[2,16,16,512]{3,2,1,0:T(8,128)S(1)}, u32[]{:S(2)}) copy-start(f32[2,16,16,512]{3,2,1,0:T(8,128)S(1)} %get-tuple-element.784) | copy-start | bytes 3145732 | tf_op jit(solution)/shard_map/while
  106.8 3.5 %copy-start.10 = (bf16[512,512]{1,0:T(8,128)(2,1)S(1)}, bf16[512,512]{1,0:T(8,128)(2,1)}, u32[]{:S(2)}) copy-start(bf16[512,512]{1,0:T(8,128)(2,1)} %get-tuple-element.911) | copy-start | bytes 1572868 | tf_op jit(solution)/shard_map/while
  106.8 3.9 %copy-start.8 = (f32[4,16,16,512]{3,2,1,0:T(8,128)S(1)}, f32[4,16,16,512]{3,2,1,0:T(8,128)}, u32[]{:S(2)}) copy-start(f32[4,16,16,512]{3,2,1,0:T(8,128)} %get-tuple-element.906) | copy-start | bytes 6291460 | tf_op jit(solution)/shard_map/while
  110.3 2.6 copy-start.2
  112.8 14.0 %collective-permute-start = (bf16[2,16,16,512]{3,2,1,0:T(8,128)(2,1)}, bf16[2,16,16,512]{3,2,1,0:T(8,128)(2,1)}, u32[]{:S(2)}, u32[]{:S(2)}) collective-permute-start(bf16[2,16,16,512]{3,2,1,0:T(8,128)(2,1)} %get-tuple-element.815), channel_id=1, source_target_pairs={{1,0},{2,1},{3,2},{5,4},{6,5},{7,6},{9,8},{10,9},{11,10},{13,12},{... | collective-permute-start | bytes 1572872 | tf_op jit(solution)/shard_map/while/body/eval_jaxpr/ppermute | solution.py:18
  117.5 5.6 %copy-start.5 = (bf16[2,16,16,512]{3,2,1,0:T(8,128)(2,1)S(1)}, bf16[2,16,16,512]{3,2,1,0:T(8,128)(2,1)}, u32[]{:S(2)}) copy-start(bf16[2,16,16,512]{3,2,1,0:T(8,128)(2,1)} %copy-done.4) | copy-start | bytes 1572868 | tf_op jit(solution)/shard_map/while
  123.1 3.1 %copy-start.3 = (bf16[2,16,16,512]{3,2,1,0:T(8,128)(2,1)S(1)}, bf16[2,16,16,512]{3,2,1,0:T(8,128)(2,1)}, u32[]{:S(2)}) copy-start(bf16[2,16,16,512]{3,2,1,0:T(8,128)(2,1)} %copy-done.2) | copy-start | bytes 1572868 | tf_op jit(solution)/shard_map/while
  123.1 3.1 %copy-start.12 = (f32[512,512]{1,0:T(8,128)S(1)}, f32[512,512]{1,0:T(8,128)}, u32[]{:S(2)}) copy-start(f32[512,512]{1,0:T(8,128)} %get-tuple-element.876) | copy-start | bytes 3145732 | tf_op jit(solution)/shard_map/while
  123.1 3.1 %copy-start.16 = (bf16[4,16,16,512]{3,2,1,0:T(8,128)(2,1)S(1)}, bf16[4,16,16,512]{3,2,1,0:T(8,128)(2,1)}, u32[]{:S(2)}) copy-start(bf16[4,16,16,512]{3,2,1,0:T(8,128)(2,1)} %get-tuple-element.912) | copy-start | bytes 3145732 | tf_op jit(solution)/shard_map/while
  127.8 4.2 %copy-start.6 = (bf16[4,16,16,512]{3,2,1,0:T(8,128)(2,1)}, bf16[4,16,16,512]{3,2,1,0:T(8,128)(2,1)S(1)}, u32[]{:S(2)}) copy-start(bf16[4,16,16,512]{3,2,1,0:T(8,128)(2,1)S(1)} %get-tuple-element.908) | copy-start | bytes 3145732 | tf_op jit(solution)/shard_map/while
  129.6 6.3 %copy-start.4 = (bf16[2,16,16,512]{3,2,1,0:T(8,128)(2,1)}, bf16[2,16,16,512]{3,2,1,0:T(8,128)(2,1)S(1)}, u32[]{:S(2)}) copy-start(bf16[2,16,16,512]{3,2,1,0:T(8,128)(2,1)S(1)} %get-tuple-element.783) | copy-start | bytes 1572868 | tf_op jit(solution)/shard_map/while
  131.9 4.0 %copy-start.1 = (f32[2,16,16,512]{3,2,1,0:T(8,128)}, f32[2,16,16,512]{3,2,1,0:T(8,128)S(1)}, u32[]{:S(2)}) copy-start(f32[2,16,16,512]{3,2,1,0:T(8,128)S(1)} %get-tuple-element.784) | copy-start | bytes 3145732 | tf_op jit(solution)/shard_map/while
  131.9 3.5 %copy-start.10 = (bf16[512,512]{1,0:T(8,128)(2,1)S(1)}, bf16[512,512]{1,0:T(8,128)(2,1)}, u32[]{:S(2)}) copy-start(bf16[512,512]{1,0:T(8,128)(2,1)} %get-tuple-element.911) | copy-start | bytes 1572868 | tf_op jit(solution)/shard_map/while
  132.0 3.9 %copy-start.8 = (f32[4,16,16,512]{3,2,1,0:T(8,128)S(1)}, f32[4,16,16,512]{3,2,1,0:T(8,128)}, u32[]{:S(2)}) copy-start(f32[4,16,16,512]{3,2,1,0:T(8,128)} %get-tuple-element.906) | copy-start | bytes 6291460 | tf_op jit(solution)/shard_map/while
  135.4 2.6 copy-start.2
  138.0 14.0 %collective-permute-start = (bf16[2,16,16,512]{3,2,1,0:T(8,128)(2,1)}, bf16[2,16,16,512]{3,2,1,0:T(8,128)(2,1)}, u32[]{:S(2)}, u32[]{:S(2)}) collective-permute-start(bf16[2,16,16,512]{3,2,1,0:T(8,128)(2,1)} %get-tuple-element.815), channel_id=1, source_target_pairs={{1,0},{2,1},{3,2},{5,4},{6,5},{7,6},{9,8},{10,9},{11,10},{13,12},{... | collective-permute-start | bytes 1572872 | tf_op jit(solution)/shard_map/while/body/eval_jaxpr/ppermute | solution.py:18
  142.6 5.6 %copy-start.5 = (bf16[2,16,16,512]{3,2,1,0:T(8,128)(2,1)S(1)}, bf16[2,16,16,512]{3,2,1,0:T(8,128)(2,1)}, u32[]{:S(2)}) copy-start(bf16[2,16,16,512]{3,2,1,0:T(8,128)(2,1)} %copy-done.4) | copy-start | bytes 1572868 | tf_op jit(solution)/shard_map/while
  148.2 3.1 %copy-start.3 = (bf16[2,16,16,512]{3,2,1,0:T(8,128)(2,1)S(1)}, bf16[2,16,16,512]{3,2,1,0:T(8,128)(2,1)}, u32[]{:S(2)}) copy-start(bf16[2,16,16,512]{3,2,1,0:T(8,128)(2,1)} %copy-done.2) | copy-start | bytes 1572868 | tf_op jit(solution)/shard_map/while
  148.2 3.1 %copy-start.12 = (f32[512,512]{1,0:T(8,128)S(1)}, f32[512,512]{1,0:T(8,128)}, u32[]{:S(2)}) copy-start(f32[512,512]{1,0:T(8,128)} %get-tuple-element.876) | copy-start | bytes 3145732 | tf_op jit(solution)/shard_map/while
  148.2 3.1 %copy-start.16 = (bf16[4,16,16,512]{3,2,1,0:T(8,128)(2,1)S(1)}, bf16[4,16,16,512]{3,2,1,0:T(8,128)(2,1)}, u32[]{:S(2)}) copy-start(bf16[4,16,16,512]{3,2,1,0:T(8,128)(2,1)} %get-tuple-element.912) | copy-start | bytes 3145732 | tf_op jit(solution)/shard_map/while
  154.2 131.8 %all-reduce.13.cloned.1.call-start = ((), (), s32[]{:S(2)}) async-start(), calls=%async_computation.1 | async-start | bytes 4194304 | tf_op jit(solution)/shard_map/psum | solution.py:168
  286.0 2.4 copy-start.14
  286.0 3.3 %copy-start.19 = (f32[1,3,3,512]{3,0,2,1:T(1,128)S(1)}, f32[1,3,3,512]{3,0,2,1:T(1,128)}, u32[]{:S(2)}) copy-start(f32[1,3,3,512]{3,0,2,1:T(1,128)} %get-tuple-element.922) | copy-start | bytes 55300
  286.0 3.9 %copy-start.18 = (f32[1,5,5,512]{3,0,2,1:T(1,128)S(1)}, f32[1,5,5,512]{3,0,2,1:T(1,128)}, u32[]{:S(2)}) copy-start(f32[1,5,5,512]{3,0,2,1:T(1,128)} %get-tuple-element.923) | copy-start | bytes 153604
  (18 other events, 23.6 us)
Sparse Core Ops, SparseCore 0:
  154.4 41.4 all-reduce.10
  198.9 87.0 all-reduce.12
where the time goes:
time: 298 us; the launch traced here: 297 us
  waiting for transfers between devices  132 us (44%)
  other arithmetic  93 us (31%)
  matrix products  34.4 us (12%)
  local copies, waits for them, and re-layouts  16 us (5%)
  between operations  14.2 us (5%)
  starting transfers between devices  6.48 us (2%)
    psum x2, waiting for transfers between devices, per_device(): lax.psum((sum_first, sum_second, sum_small, sum_large), 'dp')  131 us
    reduce_sum x10, other arithmetic, depth_conv_k(): jnp.sum(padded[:, row_tap:row_tap + height, col_tap:col_tap + width, :] *...  43.4 us
    convert_element_type x5, other arithmetic, one_step(): grad_point1 = jnp.where(part_act2 > 0, back_act2, 0.0).astype(jnp.bfloat16)  17.1 us
    dot_general x5, matrix products, one_step(): lax.dot_general(part_depth2, grad_rows, contract_first, preferred_element...  14.5 us
    dot_general x5, matrix products, one_step(): lax.dot_general(grad_rows, weight_second, contract_last, preferred_elemen...  11.8 us
    max x5, other arithmetic, one_step(): jnp.maximum(part_inputs, 0.0)  10.2 us
    select_n x5, other arithmetic, one_step(): jnp.where(section_index == section_count - 1, take(grad_last, piece_num),...  8.44 us
    unnamed x26, local copies, waits for them, and re-layouts  6.44 us
  transfers between devices with their start and end apart: 7, of which 2 were waited for; matrix products, arithmetic and copies ran while one was open for 21% of the time, Pallas kernels for 0%

commit v1 on v0

v1 whole, which is shorter than its diff:
```python
import functools

import jax
import jax.numpy as jnp
from jax import lax
from jax.experimental import pallas as pl
from jax.experimental.pallas import tpu as pltpu
from jax.sharding import PartitionSpec as P

BAND = 4
LOSS_SCALE = 64.0
LANES = 128
f32 = jnp.float32
bf16 = jnp.bfloat16
contract_last = (((1,), (1,)), ((), ()))
contract_first = (((0,), (0,)), ((), ()))


def dot(a, b, dims=(((1,), (0,)), ((), ()))):
    return lax.dot_general(a, b, dims, preferred_element_type=f32)


def split_dot(values, matrix, dims):
    rows = values.shape[0]
    high = values.astype(bf16).astype(f32)
    rest = values - high
    mid = rest.astype(bf16).astype(f32)
    low = (rest - mid).astype(bf16).astype(f32)
    parts = jnp.concatenate([high, mid, low, jnp.zeros_like(low)], axis=0).astype(bf16)
    out = dot(parts, matrix, dims)
    return out[:rows] + out[rows : 2 * rows] + out[2 * rows : 3 * rows]


def kernel(
    offsets, labels, x, k3, w1, k5, w2, head,
    grad_first, grad_second, grad_small, grad_large,
    d1, a2, d2, gin, gp1, gout, tmp, s5f, s3f, s5g, s3g, pool, pool2, acc3, acc5,
    send_sem, recv_sem,
):
    section = lax.axis_index("section")
    count = lax.axis_size("section")
    images, height, width, chans = x.shape
    rows = height * width
    blocks = chans // LANES
    last = section == count - 1
    scale = 1.0 / rows

    barrier = pltpu.get_barrier_semaphore()

    @pl.when(section > 0)
    def _():
        pl.semaphore_signal(barrier, inc=1, device_id={"section": section - 1})

    @pl.when(section < count - 1)
    def _():
        pl.semaphore_signal(barrier, inc=1, device_id={"section": section + 1})

    def cols(block):
        return pl.ds(pl.multiple_of(block * LANES, LANES), LANES)

    col_index = lax.broadcasted_iota(jnp.int32, (1, width, LANES), 1)

    def shifted(value, by):
        if by == 0:
            return value
        moved = pltpu.roll(value, (-by) % width, axis=1)
        inside = (col_index + by >= 0) & (col_index + by < width)
        return jnp.where(inside, moved, 0.0)

    def fill(ref, value, size):
        radius = size // 2
        for tap in range(size):
            ref[tap, pl.ds(radius, height)] = shifted(value, tap - radius)

    def clear(ref, size):
        radius = size // 2
        zero = jnp.zeros((radius, width, LANES), f32)
        for tap in range(size):
            ref[tap, pl.ds(0, radius)] = zero
            ref[tap, pl.ds(radius + height, radius)] = zero

    def conv(ref, weights, size, block, flip):
        total = None
        for row_tap in range(size):
            for col_tap in range(size):
                r, c = row_tap, col_tap
                if flip:
                    r, c = size - 1 - r, size - 1 - c
                tap = row_tap * size + col_tap
                part = weights[pl.ds(tap, 1), cols(block)] * ref[c, pl.ds(r, height)]
                total = part if total is None else total + part
        return total

    def kept(image):
        away = col_index - offsets[image]
        away = jnp.where(away < 0, away + width, away)
        return jnp.where((away < BAND) | (section > 0), 1.0, 0.0)

    def xin(image, block):
        return x[image, :, :, cols(block)].astype(f32) * kept(image)

    clear(s5f, 5)
    clear(s3f, 3)

    @pl.loop(0, images)
    def _(n):
        @pl.loop(0, blocks)
        def _(b):
            for ref, size in ((s5g, 5), (s3g, 3)):
                clear(ref.at[n, b], size)

    @pl.loop(0, images)
    def _(n):
        @pl.loop(0, blocks)
        def _(b):
            value = xin(n, b)
            pool[n, :, cols(b)] = jnp.sum(value.reshape(rows // 8, 8, LANES), axis=0)
            fill(s3f, jnp.maximum(value, 0.0), 3)
            out = conv(s3f, k3, 3, b, False)
            d1[n, :, cols(b)] = out.reshape(rows, LANES).astype(bf16)

        a2[n] = jnp.maximum(dot(d1[n], w1[...]), 0.0).astype(bf16)

        @pl.loop(0, blocks)
        def _(b):
            value = a2[n, :, cols(b)].astype(f32).reshape(height, width, LANES)
            fill(s5f, value, 5)
            out = conv(s5f, k5, 5, b, False).reshape(rows, LANES).astype(bf16)
            d2[n, :, cols(b)] = out
            pool2[n, :, cols(b)] = jnp.sum(
                out.astype(f32).reshape(rows // 8, 8, LANES), axis=0
            )

    @pl.when(last)
    def _():
        padded, classes = -(-images // 8) * 8, head.shape[0]

        def means(ref):
            sums = [jnp.sum(ref[n], axis=0, keepdims=True) for n in range(images)]
            sums += [jnp.zeros((1, chans), f32)] * (padded - images)
            return jnp.concatenate(sums, axis=0) * scale

        pooled = means(pool) + split_dot(means(pool2), w2[...], (((1,), (0,)), ((), ())))
        logits = split_dot(pooled, head[...], contract_last)
        row_index = lax.broadcasted_iota(jnp.int32, (padded, classes), 0)
        class_index = lax.broadcasted_iota(jnp.int32, (padded, classes), 1)
        hot = jnp.zeros((padded, classes), f32)
        for n in range(images):
            hot = jnp.where((row_index == n) & (class_index == labels[n]), 1.0, hot)
        grad = split_dot(
            LOSS_SCALE * (logits - hot), head[...], (((1,), (0,)), ((), ()))
        ) * scale
        for n in range(images):
            gin[n] = jnp.broadcast_to(grad[n : n + 1], (rows, chans)).astype(bf16)

    def hand_over(n):
        return pltpu.make_async_remote_copy(
            src_ref=gout.at[n],
            dst_ref=gin.at[n],
            send_sem=send_sem.at[n],
            recv_sem=recv_sem.at[n],
            device_id={"section": jnp.maximum(section - 1, 0)},
        )

    pl.semaphore_wait(
        barrier, jnp.where(section > 0, 1, 0) + jnp.where(section < count - 1, 1, 0)
    )

    @pl.loop(0, images)
    def _(n):
        @pl.when(jnp.logical_not(last))
        def _():
            hand_over(n).wait_recv()

        tmp[...] = dot(gin[n], w2[...], contract_last)

        @pl.loop(0, blocks)
        def _(b):
            shifts = s5g.at[n, b]
            fill(shifts, tmp[:, cols(b)].reshape(height, width, LANES), 5)
            back = conv(shifts, k5, 5, b, True).reshape(rows, LANES)
            live = a2[n, :, cols(b)].astype(f32) > 0
            gp1[n, :, cols(b)] = jnp.where(live, back, 0.0).astype(bf16)

        tmp[...] = dot(gp1[n], w1[...], contract_last)

        @pl.loop(0, blocks)
        def _(b):
            shifts = s3g.at[n, b]
            fill(shifts, tmp[:, cols(b)].reshape(height, width, LANES), 3)

            @pl.when(section > 0)
            def _():
                back = conv(shifts, k3, 3, b, True)
                back = jnp.where(xin(n, b) > 0, back, 0.0).reshape(rows, LANES)
                grad = gin[n, :, cols(b)].astype(f32) + back
                gout[n, :, cols(b)] = grad.astype(bf16)

        @pl.when(section > 0)
        def _():
            hand_over(n).start()

    flat = (images * rows, chans)
    grad_second[...] = dot(d2[...].reshape(flat), gin[...].reshape(flat), contract_first)
    grad_first[...] = dot(d1[...].reshape(flat), gp1[...].reshape(flat), contract_first)

    def kernel_grad(acc, value, ref, size):
        for row_tap in range(size):
            for col_tap in range(size):
                other = ref[size - 1 - col_tap, pl.ds(size - 1 - row_tap, height)]
                part = (value * other).reshape(rows // 8, 8, LANES)
                acc[row_tap * size + col_tap] += jnp.sum(part, axis=0)

    @pl.loop(0, blocks)
    def _(b):
        acc3[...] = jnp.zeros_like(acc3)
        acc5[...] = jnp.zeros_like(acc5)

        @pl.loop(0, images)
        def _(n):
            value = a2[n, :, cols(b)].astype(f32).reshape(height, width, LANES)
            kernel_grad(acc5, value, s5g.at[n, b], 5)
            kernel_grad(acc3, jnp.maximum(xin(n, b), 0.0), s3g.at[n, b], 3)

        grad_large[:, cols(b)] = jnp.sum(acc5[...], axis=1)
        grad_small[:, cols(b)] = jnp.sum(acc3[...], axis=1)

    @pl.when(section > 0)
    def _():
        @pl.loop(0, images)
        def _(n):
            hand_over(n).wait_send()


def per_device(
    activations, depth_small, point_first, depth_large, point_second, head_weight, offsets, labels
):
    x = activations[0]
    images, height, width, chans = x.shape
    rows = height * width
    blocks = chans // LANES
    vmem = pl.BlockSpec(memory_space=pltpu.VMEM)
    smem = pl.BlockSpec(memory_space=pltpu.SMEM)
    outs = pl.pallas_call(
        kernel,
        out_shape=(
            jax.ShapeDtypeStruct((chans, chans), f32),
            jax.ShapeDtypeStruct((chans, chans), f32),
            jax.ShapeDtypeStruct((9, chans), f32),
            jax.ShapeDtypeStruct((25, chans), f32),
        ),
        in_specs=[smem, smem] + [vmem] * 6,
        out_specs=(vmem,) * 4,
        scratch_shapes=[
            pltpu.VMEM((images, rows, chans), bf16),
            pltpu.VMEM((images, rows, chans), bf16),
            pltpu.VMEM((images, rows, chans), bf16),
            pltpu.VMEM((images, rows, chans), bf16),
            pltpu.VMEM((images, rows, chans), bf16),
            pltpu.VMEM((images, rows, chans), bf16),
            pltpu.VMEM((rows, chans), f32),
            pltpu.VMEM((5, height + 4, width, LANES), f32),
            pltpu.VMEM((3, height + 2, width, LANES), f32),
            pltpu.VMEM((images, blocks, 5, height + 4, width, LANES), f32),
            pltpu.VMEM((images, blocks, 3, height + 2, width, LANES), f32),
            pltpu.VMEM((images, 8, chans), f32),
            pltpu.VMEM((images, 8, chans), f32),
            pltpu.VMEM((9, 8, LANES), f32),
            pltpu.VMEM((25, 8, LANES), f32),
            pltpu.SemaphoreType.DMA((images,)),
            pltpu.SemaphoreType.DMA((images,)),
        ],
        compiler_params=pltpu.CompilerParams(
            collective_id=0, has_side_effects=True, vmem_limit_bytes=56 << 20
        ),
        name="sections",
    )(
        offsets,
        labels,
        x,
        depth_small[0].reshape(9, chans),
        point_first[0],
        depth_large[0].reshape(25, chans),
        point_second[0],
        head_weight,
    )
    sum_first, sum_second, sum_small, sum_large = lax.psum(outs, "dp")
    return (
        sum_first[None],
        sum_second[None],
        sum_small.reshape(1, 3, 3, chans),
        sum_large.reshape(1, 5, 5, chans),
    )


def solution(mesh):
    placed = (
        P("section", ("groups", "dp"), None, None, None),
        P("section", None, None, None),
        P("section", None, None),
        P("section", None, None, None),
        P("section", None, None),
        P(),
        P(("groups", "dp")),
        P(("groups", "dp")),
    )
    return jax.shard_map(
        per_device,
        mesh=mesh,
        in_specs=placed,
        out_specs=(
            P("section", "groups", None),
            P("section", "groups", None),
            P("section", "groups", None, None),
            P("section", "groups", None, None),
        ),
        check_vma=False,
    )
```

time: 298 us -> 195 us (0.65)
  other arithmetic: 93 us -> 0.99 us
  Pallas kernels: 0 us -> 48.5 us
  matrix products: 34.4 us -> 0 us
  waiting for transfers between devices: 132 us -> 122 us
  local copies, waits for them, and re-layouts: 16 us -> 8.98 us
  starting transfers between devices: 6.48 us -> 0.08 us
    pallas_call x0 -> x1, Pallas kernels: none -> 48.5 us  [per_device(): pl.pallas_call(kernel, out_shape=(jax.ShapeDtypeStruct((chans, chans), f3...]
    reduce_sum x10 -> x0, other arithmetic: 43.4 us -> none  [depth_conv_k(): jnp.sum(padded[:, row_tap:row_tap + height, col_tap:col_tap + width, :] *...]
    dot_general x24 -> x0, matrix products: 34.4 us -> none  [the longest x5 14.5 us: one_step(): lax.dot_general(part_depth2, grad_rows, contract_first, preferred_element...]
    convert_element_type x8 -> x0, other arithmetic: 26.5 us -> none  [the longest x5 17.1 us: one_step(): grad_point1 = jnp.where(part_act2 > 0, back_act2, 0.0).astype(jnp.bfloat16)]
    max x5 -> x0, other arithmetic: 10.2 us -> none  [one_step(): jnp.maximum(part_inputs, 0.0)]
    psum x2, waiting for transfers between devices: 131 us -> 121 us  [per_device(): sum_first, sum_second, sum_small, sum_large = lax.psum(outs, 'dp')]
    select_n x6 -> x0, other arithmetic: 9.18 us -> none  [the longest x5 8.44 us: one_step(): jnp.where(section_index == section_count - 1, take(grad_last, piece_num),...]
    ppermute x5 -> x0, starting transfers between devices: 6.4 us -> none  [from_behind(): return lax.ppermute(block, axis, route)]
  transfers between devices with their start and end apart: 7 -> 2, of which waited for: 2 -> 2; matrix products, arithmetic and copies ran while one was open for 21% -> 1% of each run, Pallas kernels for 0% -> 0%
where the time goes in v1:
time: 195 us
  waiting for transfers between devices  122 us (63%)
  Pallas kernels  48.5 us (25%)
  between operations  14.1 us (7%)
  local copies, waits for them, and re-layouts  8.98 us (5%)
    psum x2, waiting for transfers between devices, per_device(): sum_first, sum_second, sum_small, sum_large = lax.psum(outs, 'dp')  121 us
    pallas_call x1, Pallas kernels, per_device(): pl.pallas_call(kernel, out_shape=(jax.ShapeDtypeStruct((chans, chans), f3...  48.5 us
    unnamed x12, local copies, waits for them, and re-layouts  5.6 us
  transfers between devices with their start and end apart: 2, of which 2 were waited for; matrix products, arithmetic and copies ran while one was open for 1% of the time, Pallas kernels for 0%

profile of v1, /device:TPU:0, one launch (start us, length us, event | category | flops | bytes accessed | tf_op | source)
XLA Modules:
  0.0 194.7 jit_solution(2969835890893674408)
XLA Ops:
  7.2 0.0 all-reduce.5.cloned.1.call-start
  7.2 0.9 reduce.1
  8.1 0.0 copy-start.3
  8.2 0.6 reshape_squeeze.7.k5
  8.8 0.1 copy-done.3
  8.9 0.1 reduce
  8.9 0.6 reshape_squeeze.6.k3
  9.6 48.5 %sections.1 = (f32[512,512]{1,0:T(8,128)}, f32[512,512]{1,0:T(8,128)}, f32[9,512]{1,0:T(8,128)}, f32[25,512]{1,0:T(8,128)}) custom-call(s32[4]{0:T(128)} %offsets.1, s32[4]{0:T(128)} %labels.1, bf16[4,16,16,512]{3,2,1,0:T(8,128)(2,1)} %bitcast.5, f32[9,512]{1,0:T(8,128)} %reshape_squeeze.6.k3, bf16[512,512]{1,0:T(8,128)(2,1)} %bitcast.8, ...), custom_call_target="tpu_custom_call" | custom-call | tf_op jit(solution)/shard_map/sections/pallas_call | solution.py:244
  58.1 0.0 copy-start.1
  58.1 1.5 reshape.15
  59.6 0.0 copy-done.1
  59.6 0.6 reshape.14
  60.2 0.0 all-reduce.5.cloned.1.call-update
  60.2 0.0 all-reduce.7.cloned.1.call-start
  60.3 0.7 all-reduce.7.cloned.1.call-update
  61.0 33.9 %all-reduce.5.cloned.1.call-done = (f32[1,3,3,512]{3,2,1,0:T(4,128)}, f32[1,5,5,512]{3,2,1,0:T(8,128)}) async-done(((f32[1,3,3,512]{3,2,1,0:T(4,128)}, f32[1,5,5,512]{3,2,1,0:T(8,128)}), (f32[1,3,3,512]{3,2,1,0:T(4,128)}, f32[1,5,5,512]{3,2,1,0:T(8,128)})) %all-reduce.5.cloned.1.call-update) | async-done | bytes 69648 | tf_op jit(solution)/shard_map/psum | solution.py:287
  94.9 0.0 copy-start.2
  94.9 1.6 copy.15
  96.5 0.0 copy-done.2
  96.5 0.6 copy.14
  97.1 87.4 %all-reduce.7.cloned.1.call-done = (f32[1,512,512]{2,1,0:T(8,128)}, f32[1,512,512]{2,1,0:T(8,128)}) async-done(((f32[1,512,512]{2,1,0:T(8,128)}, f32[1,512,512]{2,1,0:T(8,128)}), (f32[1,512,512]{2,1,0:T(8,128)}, f32[1,512,512]{2,1,0:T(8,128)})) %all-reduce.7.cloned.1.call-update) | async-done | bytes 2097168 | tf_op jit(solution)/shard_map/psum | solution.py:287
  184.5 0.0 copy-start
  184.5 2.4 %copy.24 = f32[1,512,512]{2,1,0:T(8,128)} copy(f32[1,512,512]{2,1,0:T(8,128)} %get-tuple-element.24) | data formatting | bytes 2097152
  186.9 0.0 copy-done
  186.9 1.0 copy.25
Async XLA Ops:
  7.2 87.7 %all-reduce.5.cloned.1.call-start = ((), (), s32[]{:S(2)}) async-start(), calls=%async_computation | async-start | bytes 212992 | tf_op jit(solution)/shard_map/psum | solution.py:287
  8.1 0.7 copy-start.3
  58.1 1.5 copy-start.1
  60.2 124.3 %all-reduce.7.cloned.1.call-start = ((), (), s32[]{:S(2)}) async-start(), calls=%async_computation.1 | async-start | bytes 4194304 | tf_op jit(solution)/shard_map/psum | solution.py:287
  94.9 1.6 copy-start.2
  184.5 2.4 %copy-start = (f32[1,512,512]{2,1,0:T(8,128)S(1)}, f32[1,512,512]{2,1,0:T(8,128)}, u32[]{:S(2)}) copy-start(f32[1,512,512]{2,1,0:T(8,128)} %get-tuple-element.25) | copy-start | bytes 3145732
Sparse Core Ops, SparseCore 0:
  60.4 34.4 all-reduce.4
  97.4 87.0 all-reduce.6

commit v2 on v1

--- a/solution.py
+++ b/solution.py
@@ -1,5 +1,3 @@
-import functools
-
 import jax
 import jax.numpy as jnp
 from jax import lax
@@ -10,6 +8,8 @@
 BAND = 4
 LOSS_SCALE = 64.0
 LANES = 128
+CHUNKS = 8
+TAP_ROWS = 48
 f32 = jnp.float32
 bf16 = jnp.bfloat16
 contract_last = (((1,), (1,)), ((), ()))
@@ -31,11 +31,113 @@
     return out[:rows] + out[rows : 2 * rows] + out[2 * rows : 3 * rows]
 
 
+class Line:
+    def __init__(self, place, line, owner, refs, get, put):
+        self.place, self.line, self.owner = place, line, owner
+        self.out, self.left, self.right, self.final, self.sems = refs
+        self.get, self.put = get, put
+
+    def copy(self, k, src, dst, send, recv, step):
+        return pltpu.make_async_remote_copy(
+            src_ref=src.at[k],
+            dst_ref=dst.at[k],
+            send_sem=self.sems.at[send, k],
+            recv_sem=self.sems.at[recv, k],
+            device_id={"dp": jnp.clip(self.place + step, 0, self.line - 1)},
+        )
+
+    def to_right(self, k):
+        return self.copy(k, self.out, self.left, 0, 3, 1)
+
+    def to_left(self, k):
+        return self.copy(k, self.out, self.right, 0, 4, -1)
+
+    def final_left(self, k, src):
+        return self.copy(k, src, self.final, 1, 5, -1)
+
+    def final_right(self, k, src):
+        return self.copy(k, src, self.final, 2, 5, 1)
+
+    def relay(self, k):
+        place, line, owner, dtype = self.place, self.line, self.owner, self.out.dtype
+
+        def side(active, inner, arrival, source, send):
+            @pl.when(active & jnp.logical_not(inner))
+            def _():
+                self.out[k] = self.get(k).astype(dtype)
+
+            @pl.when(active & inner)
+            def _():
+                arrival(k).wait_recv()
+                self.out[k] = (self.get(k) + source[k].astype(f32)).astype(dtype)
+
+            @pl.when(active)
+            def _():
+                send(k).start()
+
+        side(place < owner, place > 0, self.to_right, self.left, self.to_right)
+        side(place > owner, place < line - 1, self.to_left, self.right, self.to_left)
+
+    def total(self, k):
+        line, owner, dtype = self.line, self.owner, self.out.dtype
+
+        @pl.when(self.place == owner)
+        def _():
+            value = self.get(k)
+            if owner > 0:
+                self.to_right(k).wait_recv()
+                value = value + self.left[k].astype(f32)
+            if owner < line - 1:
+                self.to_left(k).wait_recv()
+                value = value + self.right[k].astype(f32)
+            value = value.astype(dtype)
+            self.out[k] = value
+            if owner > 0:
+                self.final_left(k, self.out).start()
+            if owner < line - 1:
+                self.final_right(k, self.out).start()
+            self.put(k, value.astype(f32))
+
+    def spread(self, k):
+        place, line, owner = self.place, self.line, self.owner
+
+        @pl.when(place != owner)
+        def _():
+            self.final_left(k, self.final).wait_recv()
+
+        @pl.when((place < owner) & (place > 0))
+        def _():
+            self.final_left(k, self.final).start()
+
+        @pl.when((place > owner) & (place < line - 1))
+        def _():
+            self.final_right(k, self.final).start()
+
+        @pl.when(place != owner)
+        def _():
+            self.put(k, self.final[k].astype(f32))
+
+    def drain(self, k):
+        place, line, owner = self.place, self.line, self.owner
+
+        @pl.when(place != owner)
+        def _():
+            self.to_right(k).wait_send()
+
+        @pl.when((place <= owner) & (place > 0))
+        def _():
+            self.final_left(k, self.final).wait_send()
+
+        @pl.when((place >= owner) & (place < line - 1))
+        def _():
+            self.final_right(k, self.final).wait_send()
+
+
 def kernel(
     offsets, labels, x, k3, w1, k5, w2, head,
     grad_first, grad_second, grad_small, grad_large,
-    d1, a2, d2, gin, gp1, gout, tmp, s5f, s3f, s5g, s3g, pool, pool2, acc3, acc5,
-    send_sem, recv_sem,
+    d1, a2, d2, gin, gp1, gout, tmp, s5f, s3f, s5g, s3g, pool, pool2, acc3, acc5, taps,
+    send_sem, recv_sem, *line_refs,
 ):
     section = lax.axis_index("section")
     count = lax.axis_size("section")
@@ -55,6 +157,17 @@
     def _():
         pl.semaphore_signal(barrier, inc=1, device_id={"section": section + 1})
 
+    place = lax.axis_index("dp")
+    line = lax.axis_size("dp")
+
+    @pl.when(place > 0)
+    def _():
+        pl.semaphore_signal(barrier, inc=1, device_id={"dp": place - 1})
+
+    @pl.when(place < line - 1)
+    def _():
+        pl.semaphore_signal(barrier, inc=1, device_id={"dp": place + 1})
+
     def cols(block):
         return pl.ds(pl.multiple_of(block * LANES, LANES), LANES)
 
@@ -87,7 +200,7 @@
                 if flip:
                     r, c = size - 1 - r, size - 1 - c
                 tap = row_tap * size + col_tap
-                part = weights[pl.ds(tap, 1), cols(block)] * ref[c, pl.ds(r, height)]
+                part = weights[tap, :, cols(block)] * ref[c, pl.ds(r, height)]
                 total = part if total is None else total + part
         return total
 
@@ -163,7 +276,11 @@
         )
 
     pl.semaphore_wait(
-        barrier, jnp.where(section > 0, 1, 0) + jnp.where(section < count - 1, 1, 0)
+        barrier,
+        jnp.where(section > 0, 1, 0)
+        + jnp.where(section < count - 1, 1, 0)
+        + jnp.where(place > 0, 1, 0)
+        + jnp.where(place < line - 1, 1, 0),
     )
 
     @pl.loop(0, images)
@@ -211,8 +328,7 @@
                 part = (value * other).reshape(rows // 8, 8, LANES)
                 acc[row_tap * size + col_tap] += jnp.sum(part, axis=0)
 
-    @pl.loop(0, blocks)
-    def _(b):
+    def kernel_grads(b):
         acc3[...] = jnp.zeros_like(acc3)
         acc5[...] = jnp.zeros_like(acc5)
 
@@ -222,8 +338,74 @@
             kernel_grad(acc5, value, s5g.at[n, b], 5)
             kernel_grad(acc3, jnp.maximum(xin(n, b), 0.0), s3g.at[n, b], 3)
 
-        grad_large[:, cols(b)] = jnp.sum(acc5[...], axis=1)
-        grad_small[:, cols(b)] = jnp.sum(acc3[...], axis=1)
+        taps[0, pl.ds(0, 25), cols(b)] = jnp.sum(acc5[...], axis=1)
+        taps[0, pl.ds(32, 9), cols(b)] = jnp.sum(acc3[...], axis=1)
+
+    middle = ((line - 1) // 2, line // 2)
+    per_chunk = chans // CHUNKS
+
+    def chunk_of(ref, k):
+        return ref.at[pl.ds(pl.multiple_of(k * per_chunk, per_chunk), per_chunk)]
+
+    def put_taps(k, value):
+        for tap in range(25):
+            grad_large[tap] = value[tap : tap + 1]
+        for tap in range(9):
+            grad_small[tap] = value[32 + tap : 33 + tap]
+
+    def put_chunk(ref):
+        def put(k, value):
+            chunk_of(ref, k)[...] = value
+
+        return put
+
+    lines = (
+        Line(place, line, middle[0], line_refs[0:5],
+             lambda k: chunk_of(grad_second, k)[...], put_chunk(grad_second)),
+        Line(place, line, middle[1], line_refs[5:10],
+             lambda k: chunk_of(grad_first, k)[...], put_chunk(grad_first)),
+    )
+    tap_line = Line(place, line, middle[0], line_refs[10:15], lambda k: taps[k], put_taps)
+
+    @pl.loop(0, CHUNKS + 3)
+    def _(step):
+        @pl.when(step < CHUNKS)
+        def _():
+            for each in lines:
+                each.relay(step)
+
+        @pl.when(step < blocks)
+        def _():
+            kernel_grads(step)
+
+        @pl.when(step == blocks)
+        def _():
+            tap_line.relay(0)
+
+        @pl.when((step >= 1) & (step < CHUNKS + 1))
+        def _():
+            for each in lines:
+                each.total(step - 1)
+
+        @pl.when(step == blocks + 1)
+        def _():
+            tap_line.total(0)
+
+        @pl.when(step >= 3)
+        def _():
+            for each in lines:
+                each.spread(step - 3)
+
+        @pl.when(step == blocks + 3)
+        def _():
+            tap_line.spread(0)
+
+    tap_line.drain(0)
+
+    @pl.loop(0, CHUNKS)
+    def _(k):
+        for each in lines:
+            each.drain(k)
 
     @pl.when(section > 0)
     def _():
@@ -241,13 +423,19 @@
     blocks = chans // LANES
     vmem = pl.BlockSpec(memory_space=pltpu.VMEM)
     smem = pl.BlockSpec(memory_space=pltpu.SMEM)
-    outs = pl.pallas_call(
+
+    def line_scratch(chunks, length, dtype):
+        return [pltpu.VMEM((chunks, length, chans), dtype)] * 4 + [
+            pltpu.SemaphoreType.DMA((6, chunks))
+        ]
+
+    sum_first, sum_second, sum_small, sum_large = pl.pallas_call(
         kernel,
         out_shape=(
             jax.ShapeDtypeStruct((chans, chans), f32),
             jax.ShapeDtypeStruct((chans, chans), f32),
-            jax.ShapeDtypeStruct((9, chans), f32),
-            jax.ShapeDtypeStruct((25, chans), f32),
+            jax.ShapeDtypeStruct((9, 1, chans), f32),
+            jax.ShapeDtypeStruct((25, 1, chans), f32),
         ),
         in_specs=[smem, smem] + [vmem] * 6,
         out_specs=(vmem,) * 4,
@@ -267,8 +455,12 @@
             pltpu.VMEM((images, 8, chans), f32),
             pltpu.VMEM((9, 8, LANES), f32),
             pltpu.VMEM((25, 8, LANES), f32),
+            pltpu.VMEM((1, TAP_ROWS, chans), f32),
             pltpu.SemaphoreType.DMA((images,)),
             pltpu.SemaphoreType.DMA((images,)),
+            *line_scratch(CHUNKS, chans // CHUNKS, bf16),
+            *line_scratch(CHUNKS, chans // CHUNKS, bf16),
+            *line_scratch(1, TAP_ROWS, f32),
         ],
         compiler_params=pltpu.CompilerParams(
             collective_id=0, has_side_effects=True, vmem_limit_bytes=56 << 20
@@ -278,13 +470,12 @@
         offsets,
         labels,
         x,
-        depth_small[0].reshape(9, chans),
+        depth_small[0].reshape(9, 1, chans),
         point_first[0],
-        depth_large[0].reshape(25, chans),
+        depth_large[0].reshape(25, 1, chans),
         point_second[0],
         head_weight,
     )
-    sum_first, sum_second, sum_small, sum_large = lax.psum(outs, "dp")
     return (
         sum_first[None],
         sum_second[None],

time: 195 us -> 111 us (0.57)
  waiting for transfers between devices: 122 us -> 0 us
  Pallas kernels: 48.5 us -> 106 us
  between operations: 14.1 us -> 0.65 us
  local copies, waits for them, and re-layouts: 8.98 us -> 4.56 us
    psum x2 -> x0, waiting for transfers between devices: 121 us -> none  [per_device(): sum_first, sum_second, sum_small, sum_large = lax.psum(outs, 'dp')]
    pallas_call x1, Pallas kernels: 48.5 us -> 106 us  [per_device(): pl.pallas_call(kernel, out_shape=(jax.ShapeDtypeStruct((chans, chans), f3...]
    reshape x2 -> x0, local copies, waits for them, and re-layouts: 2.11 us -> none  [the longest x1 1.49 us: per_device(): sum_large.reshape(1, 5, 5, chans)]
    unnamed x12 -> x10, local copies, waits for them, and re-layouts: 5.6 us -> 4.56 us
  transfers between devices with their start and end apart: 2 -> 0, of which waited for: 2 -> 0; matrix products, arithmetic and copies ran while one was open for 1% -> 0% of each run, Pallas kernels for 0% -> 0%
where the time goes in v2:
time: 111 us
  Pallas kernels  106 us (95%)
  local copies, waits for them, and re-layouts  4.56 us (4%)
    pallas_call x1, Pallas kernels, per_device(): pl.pallas_call(kernel, out_shape=(jax.ShapeDtypeStruct((chans, chans), f3...  106 us
    unnamed x10, local copies, waits for them, and re-layouts  4.56 us

profile of v2, /device:TPU:0, one launch (start us, length us, event | category | flops | bytes accessed | tf_op | source)
XLA Modules:
  0.0 110.7 jit_solution(16050877439090269619)
XLA Ops:
  0.6 105.5 %sections.1 = (f32[512,512]{1,0:T(8,128)}, f32[512,512]{1,0:T(8,128)}, f32[9,1,512]{2,1,0:T(1,128)}, f32[25,1,512]{2,1,0:T(1,128)}) custom-call(s32[4]{0:T(128)} %offsets.1, s32[4]{0:T(128)} %labels.1, bf16[4,16,16,512]{3,2,1,0:T(8,128)(2,1)} %bitcast.9, f32[9,1,512]{2,1,0:T(1,128)} %bitcast.17, bf16[512,512]{1,0:T(8,128)(2,1)} %bitcast.12, ...), custom_call_target="tpu_custom_call" | custom-call | tf_op jit(solution)/shard_map/sections/pallas_call | solution.py:432
  106.1 0.0 copy-start
  106.2 2.4 %copy.16 = f32[1,512,512]{2,1,0:T(8,128)} copy(f32[1,512,512]{2,1,0:T(8,128)} %bitcast.11) | data formatting | bytes 2097152
  108.5 0.0 copy-done
  108.5 0.0 copy-start.2
  108.5 0.0 copy-start.1
  108.5 1.0 copy.17
  109.5 0.0 copy-done.2
  109.5 0.6 copy.18
  110.1 0.0 copy-done.1
  110.1 0.6 copy.19
Async XLA Ops:
  106.1 2.4 %copy-start = (f32[512,512]{1,0:T(8,128)S(1)}, f32[512,512]{1,0:T(8,128)}, u32[]{:S(2)}) copy-start(f32[512,512]{1,0:T(8,128)} %get-tuple-element.9) | copy-start | bytes 3145732
  108.5 1.0 copy-start.2
  108.5 1.6 %copy-start.1 = (f32[25,1,512]{2,1,0:T(1,128)S(1)}, f32[25,1,512]{2,1,0:T(1,128)}, u32[]{:S(2)}) copy-start(f32[25,1,512]{2,1,0:T(1,128)} %get-tuple-element.11) | copy-start | bytes 153604

commit v3 on v2

--- a/solution.py
+++ b/solution.py
@@ -9,6 +9,8 @@
 LOSS_SCALE = 64.0
 LANES = 128
 CHUNKS = 8
+LAG = 1
+UNITS = 4
 TAP_ROWS = 48
 f32 = jnp.float32
 bf16 = jnp.bfloat16
@@ -57,6 +59,22 @@
 
     def final_right(self, k, src):
         return self.copy(k, src, self.final, 2, 5, 1)
+
+    def advance(self, phase, step, chunks):
+        place, line, owner = self.place, self.line, self.owner
+        outer = jnp.where(place < owner, place, line - 1 - place)
+        apart = jnp.where(place < owner, owner - place, place - owner)
+        meet = max(owner, line - 1 - owner)
+        if phase == 0:
+            k, active, act = step - LAG * outer, place != owner, self.relay
+        elif phase == 1:
+            k, active, act = step - LAG * meet, place == owner, self.total
+        else:
+            k, active, act = step - LAG * (meet + apart), place != owner, self.spread
+
+        @pl.when(active & (k >= 0) & (k < chunks))
+        def _():
+            act(k)
 
     def relay(self, k):
         place, line, owner, dtype = self.place, self.line, self.owner, self.out.dtype
@@ -328,18 +346,22 @@
                 part = (value * other).reshape(rows // 8, 8, LANES)
                 acc[row_tap * size + col_tap] += jnp.sum(part, axis=0)
 
-    def kernel_grads(b):
-        acc3[...] = jnp.zeros_like(acc3)
-        acc5[...] = jnp.zeros_like(acc5)
-
-        @pl.loop(0, images)
-        def _(n):
-            value = a2[n, :, cols(b)].astype(f32).reshape(height, width, LANES)
-            kernel_grad(acc5, value, s5g.at[n, b], 5)
-            kernel_grad(acc3, jnp.maximum(xin(n, b), 0.0), s3g.at[n, b], 3)
-
-        taps[0, pl.ds(0, 25), cols(b)] = jnp.sum(acc5[...], axis=1)
-        taps[0, pl.ds(32, 9), cols(b)] = jnp.sum(acc3[...], axis=1)
+    def kernel_grads(unit):
+        b, n = unit // images, unit % images
+
+        @pl.when(n == 0)
+        def _():
+            acc3[...] = jnp.zeros_like(acc3)
+            acc5[...] = jnp.zeros_like(acc5)
+
+        value = a2[n, :, cols(b)].astype(f32).reshape(height, width, LANES)
+        kernel_grad(acc5, value, s5g.at[n, b], 5)
+        kernel_grad(acc3, jnp.maximum(xin(n, b), 0.0), s3g.at[n, b], 3)
+
+        @pl.when(n == images - 1)
+        def _():
+            taps[b, pl.ds(0, 25)] = jnp.sum(acc5[...], axis=1)
+            taps[b, pl.ds(32, 9)] = jnp.sum(acc3[...], axis=1)
 
     middle = ((line - 1) // 2, line // 2)
     per_chunk = chans // CHUNKS
@@ -349,9 +371,9 @@
 
     def put_taps(k, value):
         for tap in range(25):
-            grad_large[tap] = value[tap : tap + 1]
+            grad_large[tap, :, cols(k)] = value[tap : tap + 1]
         for tap in range(9):
-            grad_small[tap] = value[32 + tap : 33 + tap]
+            grad_small[tap, :, cols(k)] = value[32 + tap : 33 + tap]
 
     def put_chunk(ref):
         def put(k, value):
@@ -367,40 +389,26 @@
     )
     tap_line = Line(place, line, middle[0], line_refs[10:15], lambda k: taps[k], put_taps)
 
-    @pl.loop(0, CHUNKS + 3)
+    busy = -(-blocks * images // UNITS)
+    chunks = CHUNKS
+
+    @pl.loop(0, max(chunks, busy + blocks) + LAG * line)
     def _(step):
-        @pl.when(step < CHUNKS)
-        def _():
+        for phase in range(3):
             for each in lines:
-                each.relay(step)
-
-        @pl.when(step < blocks)
-        def _():
-            kernel_grads(step)
-
-        @pl.when(step == blocks)
-        def _():
-            tap_line.relay(0)
-
-        @pl.when((step >= 1) & (step < CHUNKS + 1))
-        def _():
-            for each in lines:
-                each.total(step - 1)
-
-        @pl.when(step == blocks + 1)
-        def _():
-            tap_line.total(0)
-
-        @pl.when(step >= 3)
-        def _():
-            for each in lines:
-                each.spread(step - 3)
-
-        @pl.when(step == blocks + 3)
-        def _():
-            tap_line.spread(0)
-
-    tap_line.drain(0)
+                each.advance(phase, step, chunks)
+            tap_line.advance(phase, step - busy, blocks)
+            if phase == 0:
+
+                @pl.when(step < busy)
+                def _():
+                    @pl.loop(0, UNITS)
+                    def _(part):
+                        kernel_grads(step * UNITS + part)
+
+    @pl.loop(0, blocks)
+    def _(k):
+        tap_line.drain(k)
 
     @pl.loop(0, CHUNKS)
     def _(k):
@@ -424,8 +432,10 @@
     vmem = pl.BlockSpec(memory_space=pltpu.VMEM)
     smem = pl.BlockSpec(memory_space=pltpu.SMEM)
 
-    def line_scratch(chunks, length, dtype):
-        return [pltpu.VMEM((chunks, length, chans), dtype)] * 4 + [
+    link = bf16 if lax.axis_size("dp") <= 4 else f32
+
+    def line_scratch(chunks, length, wide, dtype):
+        return [pltpu.VMEM((chunks, length, wide), dtype)] * 4 + [
             pltpu.SemaphoreType.DMA((6, chunks))
         ]
 
@@ -455,12 +465,12 @@
             pltpu.VMEM((images, 8, chans), f32),
             pltpu.VMEM((9, 8, LANES), f32),
             pltpu.VMEM((25, 8, LANES), f32),
-            pltpu.VMEM((1, TAP_ROWS, chans), f32),
+            pltpu.VMEM((blocks, TAP_ROWS, LANES), f32),
             pltpu.SemaphoreType.DMA((images,)),
             pltpu.SemaphoreType.DMA((images,)),
-            *line_scratch(CHUNKS, chans // CHUNKS, bf16),
-            *line_scratch(CHUNKS, chans // CHUNKS, bf16),
-            *line_scratch(1, TAP_ROWS, f32),
+            *line_scratch(CHUNKS, chans // CHUNKS, chans, link),
+            *line_scratch(CHUNKS, chans // CHUNKS, chans, link),
+            *line_scratch(blocks, TAP_ROWS, LANES, f32),
         ],
         compiler_params=pltpu.CompilerParams(
             collective_id=0, has_side_effects=True, vmem_limit_bytes=56 << 20

time: 111 us -> 86.6 us (0.78)
  Pallas kernels: 106 us -> 81.2 us
    pallas_call x1, Pallas kernels: 106 us -> 81.2 us  [per_device(): pl.pallas_call(kernel, out_shape=(jax.ShapeDtypeStruct((chans, chans), f3...]
where the time goes in v3:
time: 86.6 us; the launch traced here: 86.4 us
  Pallas kernels  81.2 us (94%)
  local copies, waits for them, and re-layouts  4.56 us (5%)
    pallas_call x1, Pallas kernels, per_device(): pl.pallas_call(kernel, out_shape=(jax.ShapeDtypeStruct((chans, chans), f3...  81.2 us
    unnamed x10, local copies, waits for them, and re-layouts  4.56 us

profile of v3, /device:TPU:0, one launch (start us, length us, event | category | flops | bytes accessed | tf_op | source)
XLA Modules:
  0.0 86.4 jit_solution(12802629276948387270)
XLA Ops:
  0.6 81.2 %sections.1 = (f32[512,512]{1,0:T(8,128)}, f32[512,512]{1,0:T(8,128)}, f32[9,1,512]{2,1,0:T(1,128)}, f32[25,1,512]{2,1,0:T(1,128)}) custom-call(s32[4]{0:T(128)} %offsets.1, s32[4]{0:T(128)} %labels.1, bf16[4,16,16,512]{3,2,1,0:T(8,128)(2,1)} %bitcast.9, f32[9,1,512]{2,1,0:T(1,128)} %bitcast.17, bf16[512,512]{1,0:T(8,128)(2,1)} %bitcast.12, ...), custom_call_target="tpu_custom_call" | custom-call | tf_op jit(solution)/shard_map/sections/pallas_call | solution.py:442
  81.9 0.0 copy-start
  81.9 2.4 %copy.16 = f32[1,512,512]{2,1,0:T(8,128)} copy(f32[1,512,512]{2,1,0:T(8,128)} %bitcast.11) | data formatting | bytes 2097152
  84.2 0.0 copy-done
  84.2 0.0 copy-start.2
  84.2 0.0 copy-start.1
  84.2 1.0 %copy.17 = f32[1,512,512]{2,1,0:T(8,128)} copy(f32[1,512,512]{2,1,0:T(8,128)S(1)} %bitcast.10) | data formatting | bytes 2097152
  85.2 0.0 copy-done.2
  85.2 0.6 copy.18
  85.8 0.0 copy-done.1
  85.8 0.6 copy.19
Async XLA Ops:
  81.9 2.4 %copy-start = (f32[512,512]{1,0:T(8,128)S(1)}, f32[512,512]{1,0:T(8,128)}, u32[]{:S(2)}) copy-start(f32[512,512]{1,0:T(8,128)} %get-tuple-element.9) | copy-start | bytes 3145732
  84.2 1.0 %copy-start.2 = (f32[9,1,512]{2,1,0:T(1,128)S(1)}, f32[9,1,512]{2,1,0:T(1,128)}, u32[]{:S(2)}) copy-start(f32[9,1,512]{2,1,0:T(1,128)} %get-tuple-element.10) | copy-start | bytes 55300
  84.2 1.6 %copy-start.1 = (f32[25,1,512]{2,1,0:T(1,128)S(1)}, f32[25,1,512]{2,1,0:T(1,128)}, u32[]{:S(2)}) copy-start(f32[25,1,512]{2,1,0:T(1,128)} %get-tuple-element.11) | copy-start | bytes 153604
